TPU v7x, 32 devices: a whole 2x2x4 slice. The times are simulated.
32 devices in a mesh: aa: 8 (over y, x, core), ba: 4 (over z).
Axes of the slice: x: 2, y: 2, z: 4, core: 2. Of those that a mesh axis runs over, the one named last changes fastest.
Arguments:
- amplitudes: bfloat16 [1024, 2048], P('ba', 'aa'), may hold values from -6 to 6
- integrals: bfloat16 [512, 512, 2048], P('aa', 'ba'), may hold values from -0.125 to 0.125
- virt_energy: float32 [512], replicated, may hold values from 0.2 to 2
- pair_energy: float32 [1024], replicated, may hold values from 0.3 to 3
Outputs:
- update: float32 [512, 512, 1024], P('aa', 'ba')
All inputs are finite; a program needn't handle non-finite values.
Results may differ from a plain program's by a relative error of at most 0.0003.
Values may be sent and summed in bfloat16 or wider, within the bound.
A program may use at most 128 MiB of HBM per device.

v0:
```python
import jax
import jax.numpy as jnp
from jax import lax
from jax.sharding import PartitionSpec as P


def contract(left, right):
    return lax.dot_general(
        left, right, (((1,), (1,)), ((), ())), preferred_element_type=jnp.float32
    )


def on_device(amplitudes, integrals, virt_energy, pair_energy):
    first_count = integrals.shape[0]
    second_count = integrals.shape[1]
    cd_count = integrals.shape[2]
    flat_ints = integrals.reshape(first_count * second_count, cd_count)
    all_rows = lax.all_gather(amplitudes, "ba", axis=0, tiled=True)
    whole = lax.all_gather(all_rows, "aa", axis=1, tiled=True)
    ladder = contract(flat_ints, whole)
    pair_total = ladder.shape[1]
    ladder = ladder.reshape(first_count, second_count, pair_total)
    first_energy = lax.dynamic_slice_in_dim(
        virt_energy, lax.axis_index("aa") * first_count, first_count, 0
    )
    second_energy = lax.dynamic_slice_in_dim(
        virt_energy, lax.axis_index("ba") * second_count, second_count, 0
    )
    denom = first_energy[:, None, None] + second_energy[None, :, None] + pair_energy[None, None, :]
    return ladder / denom


def solution(mesh):
    placed = (P("ba", "aa"), P("aa", "ba", None), P(), P())
    return jax.shard_map(
        on_device, mesh=mesh, in_specs=placed, out_specs=P("aa", "ba", None), check_vma=False
    )
```

profile of v0, /device:TPU:0, one launch (start us, length us, event | category | flops | bytes accessed | tf_op | source)
XLA Modules:
  0.0 112.0 jit_solution(7729294179379284813)
XLA Ops:
  6.5 0.0 all-gather.2.cloned.1.call-start
  6.5 19.4 %all_gather.6 = bf16[1024,256]{1,0:T(8,128)(2,1)} all-gather(bf16[256,256]{1,0:T(8,128)(2,1)} %param.4), channel_id=1, replica_groups=mesh['aa'=8,'ba'=4] {'ba'}, dimensions={0}, use_global_device_ids=true | all-gather | bytes 655360 | tf_op jit(solution)/shard_map/all_gather | solution.py:18
  25.9 0.0 all-gather.2.cloned.1.call-update
  25.9 0.8 dynamic_slice.7
  26.7 0.8 dynamic_slice.6
  27.4 0.1 broadcast_add_fusion
  27.5 35.6 %all-gather.2.cloned.1.call-done = bf16[1024,2048]{1,0:T(8,128)(2,1)} async-done(((bf16[1024,256]{1,0:T(8,128)(2,1)}), bf16[1024,2048]{1,0:T(8,128)(2,1)}) %all-gather.2.cloned.1.call-update) | async-done | bytes 4194320 | tf_op jit(solution)/shard_map/all_gather | solution.py:19
  63.1 42.0 %add_divide_fusion = f32[64,128,1024]{2,1,0:T(8,128)} fusion(f32[1024]{0:T(1024)} %param.7, f32[64,128]{1,0:T(8,128)S(1)} %broadcast_add_fusion, bf16[64,128,2048]{2,1,0:T(8,128)(2,1)} %param.5, bf16[1024,2048]{1,0:T(8,128)(2,1)} %all-gather.2.cloned.1.call-done), kind=kOutput, calls=%fused_computation | convolution fusion | flops 34376515584 | bytes 71340032 | tf_op jit(solution)/shard_map/dot_general | solution.py:8
Async XLA Ops:
  6.5 56.6 %all-gather.2.cloned.1.call-start = ((), (), s32[]{:S(2)}) async-start(), calls=%async_computation | async-start | bytes 4718592 | tf_op jit(solution)/shard_map/all_gather | solution.py:19
Sparse Core Ops, SparseCore 0:
  26.0 37.0 all-gather.1
where the time goes:
time: 112 us
  matrix products  42 us (38%)
  waiting for transfers between devices  35.6 us (32%)
  blocking collectives  19.4 us (17%)
  between operations  13.4 us (12%)
  local copies, waits for them, and re-layouts  1.51 us (1%)
    dot_general x1, matrix products, contract(): lax.dot_general(left, right, (((1,), (1,)), ((), ())), preferred_element_...  42 us
    all_gather x1, waiting for transfers between devices, on_device(): whole = lax.all_gather(all_rows, 'aa', axis=1, tiled=True)  35.6 us
    all_gather x1, blocking collectives, on_device(): all_rows = lax.all_gather(amplitudes, 'ba', axis=0, tiled=True)  19.4 us
  transfers between devices with their start and end apart: 1, of which 1 were waited for; matrix products, arithmetic and copies ran while one was open for 1% of the time, Pallas kernels for 0%

commit v1 on v0

--- a/solution.py
+++ b/solution.py
@@ -16,7 +16,15 @@
     cd_count = integrals.shape[2]
     flat_ints = integrals.reshape(first_count * second_count, cd_count)
     all_rows = lax.all_gather(amplitudes, "ba", axis=0, tiled=True)
-    whole = lax.all_gather(all_rows, "aa", axis=1, tiled=True)
+    ways, here = (lax.axis_size("aa"), lax.axis_index("aa"))
+    grown, reach = (all_rows, 1)
+    while reach < ways:
+        theirs = lax.ppermute(grown, "aa", [(d, d ^ reach) for d in range(ways)])
+        mine_first = jnp.concatenate([grown, theirs], axis=1)
+        theirs_first = jnp.concatenate([theirs, grown], axis=1)
+        grown = jnp.where(here & reach == 0, mine_first, theirs_first)
+        reach = 2 * reach
+    whole = grown
     ladder = contract(flat_ints, whole)
     pair_total = ladder.shape[1]
     ladder = ladder.reshape(first_count, second_count, pair_total)

time: 112 us -> 195 us (1.74)
  waiting for transfers between devices: 35.6 us -> 70.9 us
  local copies, waits for them, and re-layouts: 1.51 us -> 33.6 us
  other arithmetic: 0.07 us -> 26.2 us
  between operations: 13.4 us -> 0.02 us
  starting transfers between devices: 0.01 us -> 3.14 us
    ppermute x0 -> x3, waiting for transfers between devices: none -> 70.9 us  [on_device(): theirs = lax.ppermute(grown, 'aa', [(d, d ^ reach) for d in range(ways)])]
    all_gather x1 -> x0, waiting for transfers between devices: 35.6 us -> none  [on_device(): whole = lax.all_gather(all_rows, 'aa', axis=1, tiled=True)]
    reshape x0 -> x1, local copies, waits for them, and re-layouts: none -> 33.5 us  [on_device(): ladder = ladder.reshape(first_count, second_count, pair_total)]
    div x0 -> x1, other arithmetic: none -> 23.6 us  [on_device(): return ladder / denom]
    ppermute x0 -> x3, starting transfers between devices: none -> 3.14 us  [on_device(): theirs = lax.ppermute(grown, 'aa', [(d, d ^ reach) for d in range(ways)])]
    select_n x0 -> x2, other arithmetic: none -> 2.53 us  [on_device(): grown = jnp.where(here & reach == 0, mine_first, theirs_first)]
  transfers between devices with their start and end apart: 1 -> 3, of which waited for: 1 -> 3; matrix products, arithmetic and copies ran while one was open for 1% -> 0% of each run, Pallas kernels for 0% -> 0%
where the time goes in v1:
time: 195 us; the launch traced here: 194 us
  waiting for transfers between devices  70.9 us (36%)
  matrix products  42.8 us (22%)
  local copies, waits for them, and re-layouts  33.6 us (17%)
  other arithmetic  26.2 us (13%)
  blocking collectives  17.7 us (9%)
  starting transfers between devices  3.14 us (2%)
    ppermute x3, waiting for transfers between devices, on_device(): theirs = lax.ppermute(grown, 'aa', [(d, d ^ reach) for d in range(ways)])  70.9 us
    dot_general x1, matrix products, contract(): lax.dot_general(left, right, (((1,), (1,)), ((), ())), preferred_element_...  42.8 us
    reshape x1, local copies, waits for them, and re-layouts, on_device(): ladder = ladder.reshape(first_count, second_count, pair_total)  33.5 us
    div x1, other arithmetic, on_device(): return ladder / denom  23.6 us
    all_gather x1, blocking collectives, on_device(): all_rows = lax.all_gather(amplitudes, 'ba', axis=0, tiled=True)  17.7 us
  transfers between devices with their start and end apart: 3, of which 3 were waited for; matrix products, arithmetic and copies ran while one was open for 0% of the time, Pallas kernels for 0%

profile of v1, /device:TPU:0, one launch (start us, length us, event | category | flops | bytes accessed | tf_op | source)
XLA Modules:
  0.0 194.4 jit_solution(3778121088974256673)
XLA Ops:
  0.0 0.0 copy-start.1
  0.0 17.7 %all_gather.3 = bf16[1024,256]{1,0:T(8,128)(2,1)S(1)} all-gather(bf16[256,256]{1,0:T(8,128)(2,1)} %param.4), channel_id=1, replica_groups=mesh['aa'=8,'ba'=4] {'ba'}, dimensions={0}, use_global_device_ids=true | all-gather | bytes 655360 | tf_op jit(solution)/shard_map/all_gather | solution.py:18
  17.7 0.0 collective-permute-start
  17.7 1.9 collective-permute-done
  19.6 0.2 maximum_select_fusion.3
  19.9 1.6 collective-permute-start.1
  21.4 23.8 %collective-permute-done.1 = bf16[1024,512]{1,0:T(8,128)(2,1)} collective-permute-done((bf16[1024,512]{1,0:T(8,128)(2,1)S(1)}, bf16[1024,512]{1,0:T(8,128)(2,1)}, u32[]{:S(2)}, u32[]{:S(2)}) %collective-permute-start.1) | collective-permute-done | bytes 1048608 | tf_op jit(solution)/shard_map/ppermute | solution.py:22
  45.2 2.3 %maximum_select_fusion.2 = bf16[1024,1024]{1,0:T(8,128)(2,1)S(1)} fusion(bf16[1024,512]{1,0:T(8,128)(2,1)} %collective-permute-done.1, bf16[1024,512]{1,0:T(8,128)(2,1)S(1)} %maximum_select_fusion.3, pred[]{:T(512)S(6)} %eq.10), kind=kLoop, calls=%fused_computation.9 | loop fusion | flops 9437184 | bytes 4194305 | tf_op jit(solution)/shard_map/jit(_where)/select_n | solution.py:25
  47.5 1.6 collective-permute-start.2
  49.1 0.0 copy-done.1
  49.1 0.1 dynamic_slice.7
  49.2 0.1 dynamic_slice.6
  49.3 0.1 broadcast_add_fusion
  49.3 45.2 %collective-permute-done.2 = bf16[1024,1024]{1,0:T(8,128)(2,1)} collective-permute-done((bf16[1024,1024]{1,0:T(8,128)(2,1)S(1)}, bf16[1024,1024]{1,0:T(8,128)(2,1)}, u32[]{:S(2)}, u32[]{:S(2)}) %collective-permute-start.2) | collective-permute-done | bytes 2097184 | tf_op jit(solution)/shard_map/ppermute | solution.py:22
  94.5 42.8 %convolution_bitcast_fusion = f32[8192,1024]{0,1:T(8,128)} fusion(bf16[8192,2048]{1,0:T(8,128)(2,1)} %bitcast.6, bf16[1024,1024]{1,0:T(8,128)(2,1)} %collective-permute-done.2, bf16[1024,1024]{1,0:T(8,128)(2,1)S(1)} %maximum_select_fusion.2, pred[]{:T(512)S(6)} %eq.9), kind=kOutput, calls=%fused_computation.1 | convolution fusion | flops 34378612736 | bytes 71303168 | tf_op jit(solution)/shard_map/dot_general | solution.py:8
  137.3 0.0 copy-start
  137.3 33.5 %copy.6 = f32[8192,1024]{1,0:T(8,128)} copy(f32[8192,1024]{0,1:T(8,128)} %convolution_bitcast_fusion) | data formatting | bytes 67108864 | tf_op jit(solution)/shard_map/reshape | solution.py:30
  170.8 0.0 copy-done
  170.8 23.6 %add_divide_fusion = f32[64,128,1024]{2,1,0:T(8,128)} fusion(f32[64,128,1024]{2,1,0:T(8,128)} %bitcast.5, f32[1024]{0:T(1024)S(1)} %copy-done, f32[64,128]{1,0:T(8,128)S(1)} %broadcast_add_fusion), kind=kLoop, calls=%fused_computation | loop fusion | flops 16777216 | bytes 67145728 | tf_op jit(solution)/shard_map/div | solution.py:38
Async XLA Ops:
  0.0 49.1 %copy-start.1 = (f32[512]{0:T(512)S(1)}, f32[512]{0:T(512)}, u32[]{:S(2)}) copy-start(f32[512]{0:T(512)} %param.6) | copy-start | bytes 6148
  17.7 1.9 collective-permute-start
  19.9 25.4 %collective-permute-start.1 = (bf16[1024,512]{1,0:T(8,128)(2,1)S(1)}, bf16[1024,512]{1,0:T(8,128)(2,1)}, u32[]{:S(2)}, u32[]{:S(2)}) collective-permute-start(bf16[1024,512]{1,0:T(8,128)(2,1)S(1)} %maximum_select_fusion.3), channel_id=1, source_target_pairs={{0,8},{4,12},{8,0},{12,4},{16,24},{20,28},{24,16},{28,20},{1,9},{5... | collective-permute-start | bytes 3145736 | tf_op jit(solution)/shard_map/ppermute | solution.py:22
  47.5 47.0 %collective-permute-start.2 = (bf16[1024,1024]{1,0:T(8,128)(2,1)S(1)}, bf16[1024,1024]{1,0:T(8,128)(2,1)}, u32[]{:S(2)}, u32[]{:S(2)}) collective-permute-start(bf16[1024,1024]{1,0:T(8,128)(2,1)S(1)} %maximum_select_fusion.2), channel_id=1, source_target_pairs={{0,16},{4,20},{8,24},{12,28},{16,0},{20,4},{24,8},{28,12},{1,17},{... | collective-permute-start | bytes 6291464 | tf_op jit(solution)/shard_map/ppermute | solution.py:22
  137.3 33.5 %copy-start = (f32[1024]{0:T(1024)S(1)}, f32[1024]{0:T(1024)}, u32[]{:S(2)}) copy-start(f32[1024]{0:T(1024)} %param.7) | copy-start | bytes 12292
